TPU v7x, 32 devices: a whole 2x2x4 slice. The times are simulated.
32 devices in a mesh: row: 8 (over z, x), col: 4 (over y, core).
Axes of the slice: x: 2, y: 2, z: 4, core: 2. Of those that a mesh axis runs over, the one named last changes fastest.
Arguments:
- features: bfloat16 [14336, 2048], P('row', 'col'), may hold values from -6 to 6
- neighbours: int32 [14336, 32], P('row'), may hold values from -1 to 127, as said below
- node_valid: int32 [14336], P('row'), may hold values from 0 to 1, as said below
- weight_one: bfloat16 [2048, 2048], P(None, 'col'), may hold values from -0.125 to 0.125
- gamma_one: float32 [2048], P('col'), may hold values from 0.25 to 1.75
- beta_one: float32 [2048], P('col'), may hold values from -0.5 to 0.5
- weight_two: bfloat16 [2048, 2048], P(None, 'col'), may hold values from -0.125 to 0.125
- gamma_two: float32 [2048], P('col'), may hold values from 0.25 to 1.75
- beta_two: float32 [2048], P('col'), may hold values from -0.5 to 0.5
- cotangent: bfloat16 [14336, 2048], P('row', 'col'), may hold values from -6 to 6
Outputs:
- output: float32 [14336, 2048], P('row', 'col')
- grad_features: float32 [14336, 2048], P('row', 'col')
- grad_weight_one: float32 [2048, 2048], P(None, 'col')
- grad_gamma_one: float32 [2048], P('col')
- grad_beta_one: float32 [2048], P('col')
- grad_weight_two: float32 [2048, 2048], P(None, 'col')
- grad_gamma_two: float32 [2048], P('col')
- grad_beta_two: float32 [2048], P('col')
Inputs may be any that keep to these rules, and one draw needn't show every extreme that they name: `neighbours`: entries >= 0 name valid nodes of the same slot; every valid node has 1 to 32 such entries, first in its list, the rest are -1; a padding row has only -1; some slot is full. `node_valid`: in each slot the valid nodes come first and number at least 40.
All inputs are finite; a program needn't handle non-finite values.
Results may differ from a plain program's by a relative error of at most 0.012.
Values may be sent and summed in bfloat16 or wider, within the bound.
No kernel may reach another device: no remote copies, remote signals or barrier semaphores. Data moves between devices by JAX's collectives and lax.ppermute only.
A program may use at most 128 MiB of HBM per device.

v0:
```python
import jax
import jax.numpy as jnp
from jax import lax
from jax.sharding import PartitionSpec as P

SLOT = 128
NBR = 32
EPSILON = 1e-05


def build_tiles(neighbours):
    entries_all = neighbours.reshape(-1, SLOT, NBR)

    def build(entries):
        columns = jnp.arange(SLOT, dtype=jnp.int32)
        hits = jnp.sum((entries[:, :, None] == columns[None, None, :]).astype(jnp.float32), axis=1)
        degree = jnp.sum((entries >= 0).astype(jnp.float32), axis=1)
        joined = hits + jnp.eye(SLOT, dtype=jnp.float32)
        return joined / (degree[:, None] + 1.0)

    tiles = lax.map(build, entries_all)
    return (tiles, jnp.diagonal(tiles, axis1=1, axis2=2))


def spread(values, tiles, self_weight):
    shaped = values.reshape(tiles.shape[0], SLOT, values.shape[1])
    summed = jnp.einsum("sij,sjd->sid", tiles, shaped, precision=lax.Precision.HIGHEST)
    return (summed + self_weight[:, :, None] * shaped).reshape(values.shape)


def spread_back(grads, tiles, self_weight):
    shaped = grads.reshape(tiles.shape[0], SLOT, grads.shape[1])
    summed = jnp.einsum("sji,sjd->sid", tiles, shaped, precision=lax.Precision.HIGHEST)
    return (summed + self_weight[:, :, None] * shaped).reshape(grads.shape)


def moments(linear, valid):
    total_valid, summed = lax.psum((jnp.sum(valid), jnp.sum(valid * linear, axis=0)), "row")
    mean = summed / total_valid
    centred = linear - mean
    variance = lax.psum(jnp.sum(valid * centred * centred, axis=0), "row") / total_valid
    return (total_valid, mean, variance)


def forward_layer(values, weight, gamma, beta, tiles, self_weight, valid):
    mixed = spread(values, tiles, self_weight).astype(jnp.bfloat16)
    gathered = lax.all_gather(mixed, "col", axis=1, tiled=True)
    linear = jnp.dot(gathered, weight, preferred_element_type=jnp.float32)
    total_valid, mean, variance = moments(linear, valid)
    inv_std = lax.rsqrt(variance + EPSILON)
    normed = (linear - mean) * inv_std
    before = gamma * normed + beta
    result = valid * jax.nn.silu(before)
    return (result, (gathered, normed, inv_std, before, total_valid))


def backward_layer(grad_result, weight, gamma, kept, tiles, self_weight, valid):
    gathered, normed, inv_std, before, total_valid = kept
    sigmoid_value = jax.nn.sigmoid(before)
    slope = sigmoid_value * (1.0 + before * (1.0 - sigmoid_value))
    grad_before = grad_result * valid * slope
    grad_beta, grad_gamma = lax.psum(
        (jnp.sum(grad_before, axis=0), jnp.sum(grad_before * normed, axis=0)), "row"
    )
    grad_normed = gamma * grad_before
    grad_linear = inv_std * (
        grad_normed - valid * (gamma * grad_beta + normed * gamma * grad_gamma) / total_valid
    )
    grad_low = grad_linear.astype(jnp.bfloat16)
    weight_terms = lax.dot_general(
        gathered, grad_low, (((0,), (0,)), ((), ())), preferred_element_type=jnp.float32
    )
    grad_weight = lax.psum(weight_terms, "row")
    partial_terms = lax.dot_general(
        grad_low, weight, (((1,), (1,)), ((), ())), preferred_element_type=jnp.float32
    )
    grad_mixed = lax.psum_scatter(partial_terms, "col", scatter_dimension=1, tiled=True)
    grad_values = spread_back(grad_mixed, tiles, self_weight)
    return (grad_values, grad_weight, grad_gamma, grad_beta)


def local(
    features,
    neighbours,
    node_valid,
    weight_one,
    gamma_one,
    beta_one,
    weight_two,
    gamma_two,
    beta_two,
    cotangent,
):
    tiles, self_weight = build_tiles(neighbours)
    valid = node_valid.astype(jnp.float32)[:, None]
    hidden, kept_one = forward_layer(
        features.astype(jnp.float32), weight_one, gamma_one, beta_one, tiles, self_weight, valid
    )
    output, kept_two = forward_layer(
        hidden, weight_two, gamma_two, beta_two, tiles, self_weight, valid
    )
    grad_hidden, grad_weight_two, grad_gamma_two, grad_beta_two = backward_layer(
        cotangent.astype(jnp.float32), weight_two, gamma_two, kept_two, tiles, self_weight, valid
    )
    grad_features, grad_weight_one, grad_gamma_one, grad_beta_one = backward_layer(
        grad_hidden, weight_one, gamma_one, kept_one, tiles, self_weight, valid
    )
    return (
        output,
        grad_features,
        grad_weight_one,
        grad_gamma_one,
        grad_beta_one,
        grad_weight_two,
        grad_gamma_two,
        grad_beta_two,
    )


def solution(mesh):
    placed = (
        P("row", "col"),
        P("row", None),
        P("row"),
        P(None, "col"),
        P("col"),
        P("col"),
        P(None, "col"),
        P("col"),
        P("col"),
        P("row", "col"),
    )
    return jax.shard_map(
        local,
        mesh=mesh,
        in_specs=placed,
        out_specs=(
            P("row", "col"),
            P("row", "col"),
            P(None, "col"),
            P("col"),
            P("col"),
            P(None, "col"),
            P("col"),
            P("col"),
        ),
        check_vma=False,
    )
```

profile of v0, /device:TPU:0, one launch (start us, length us, event | category | flops | bytes accessed | tf_op | source)
XLA Modules:
  0.0 855.5 jit_solution(2408295498759646820)
XLA Ops:
  7.3 2.3 copy.23
  9.6 27.6 %while.10 = (s32[]{:T(128)}, f32[14,128,128]{2,1,0:T(8,128)S(1)}, s32[14,128,32]{2,1,0:T(8,128)}, s32[]{:T(128)}) while((s32[]{:T(128)}, f32[14,128,128]{2,1,0:T(8,128)S(1)}, s32[14,128,32]{2,1,0:T(8,128)}, s32[]{:T(128)}) %tuple.47), condition=%wide.region_3.4_spmd, body=%wide.region_0.3_spmd.sunk | while | flops 1634306 | bytes 247877 | solution.py:21
  11.5 0.9 convert_reduce_fusion.5
  13.5 0.9 convert_reduce_fusion.5
  15.5 0.9 convert_reduce_fusion.5
  17.4 0.9 convert_reduce_fusion.5
  19.4 0.9 convert_reduce_fusion.5
  21.4 0.9 convert_reduce_fusion.5
  23.4 0.9 convert_reduce_fusion.5
  25.3 0.9 convert_reduce_fusion.5
  27.3 0.9 convert_reduce_fusion.5
  29.3 0.9 convert_reduce_fusion.5
  31.3 0.9 convert_reduce_fusion.5
  33.2 0.9 convert_reduce_fusion.5
  37.2 4.7 copy.24
  41.8 1.8 gather_fusion
  43.7 5.1 add_convert_fusion.1
  49.5 54.5 %all-gather.3.cloned.1.call-done = bf16[1792,2048]{1,0:T(8,128)(2,1)} async-done(((bf16[1792,512]{1,0:T(8,128)(2,1)}), bf16[1792,2048]{1,0:T(8,128)(2,1)}) %all-gather.3.cloned.1.call-update) | async-done | bytes 7340048 | tf_op jit(solution)/shard_map/all_gather | solution.py:47
  104.0 9.5 %multiply_reduce_fusion.3 = (f32[512]{0:T(512)S(1)}, f32[1792,512]{1,0:T(8,128)}) fusion(f32[1792]{0:T(1024)S(1)} %convert_element_type.41, bf16[1792,2048]{1,0:T(8,128)(2,1)} %all-gather.3.cloned.1.call-done, bf16[2048,512]{1,0:T(8,128)(2,1)} %param.15), kind=kOutput, calls=%fused_computation.29 | convolution fusion | flops 3759930880 | bytes 13116416 | tf_op jit(solution)/shard_map/dot_general | solution.py:48
  113.5 22.0 %all-reduce.2 = (f32[512]{0:T(512)S(1)}, f32[]{:T(128)}) all-reduce(f32[512]{0:T(512)S(1)} %get-tuple-element.49, f32[]{:T(128)} %convert_reduce_fusion.2), channel_id=1, replica_groups=mesh['row'=8,'col'=4] {'row'}, use_global_device_ids=true, to_apply=%region_5.6 | all-reduce | flops 513 | bytes 4104 | tf_op jit(solution)/shard_map/psum | solution.py:38
  136.0 2.6 fusion.2
  138.6 17.1 %psum.82 = f32[512]{0:T(512)S(1)} all-reduce(f32[512]{0:T(512)S(1)} %fusion.2), channel_id=1, replica_groups=mesh['row'=8,'col'=4] {'row'}, use_global_device_ids=true, to_apply=%region_9.10 | all-reduce | flops 512 | bytes 4096 | tf_op jit(solution)/shard_map/psum | solution.py:41
  156.3 3.0 multiply_multiply_fusion.4
  159.4 4.5 add_convert_fusion
  164.1 50.0 %all-gather.5.cloned.1.call-done = bf16[1792,2048]{1,0:T(8,128)(2,1)} async-done(((bf16[1792,512]{1,0:T(8,128)(2,1)}), bf16[1792,2048]{1,0:T(8,128)(2,1)}) %all-gather.5.cloned.1.call-update) | async-done | bytes 7340048 | tf_op jit(solution)/shard_map/all_gather | solution.py:47
  214.1 8.9 %multiply_reduce_fusion.2 = (f32[512]{0:T(512)S(1)}, f32[1792,512]{1,0:T(8,128)}) fusion(f32[1792]{0:T(1024)S(1)} %convert_element_type.41, bf16[1792,2048]{1,0:T(8,128)(2,1)} %all-gather.5.cloned.1.call-done, bf16[2048,512]{1,0:T(8,128)(2,1)S(1)} %copy-done), kind=kOutput, calls=%fused_computation.25 | convolution fusion | flops 3759930880 | bytes 13116416 | tf_op jit(solution)/shard_map/dot_general | solution.py:48
  223.0 21.5 %psum.83 = f32[512]{0:T(512)S(1)} all-reduce(f32[512]{0:T(512)S(1)} %get-tuple-element.51), channel_id=1, replica_groups=mesh['row'=8,'col'=4] {'row'}, use_global_device_ids=true, to_apply=%region_11.12 | all-reduce | flops 512 | bytes 4096 | tf_op jit(solution)/shard_map/psum | solution.py:38
  245.1 2.6 fusion.3
  247.7 17.1 %psum.84 = f32[512]{0:T(512)S(1)} all-reduce(f32[512]{0:T(512)S(1)} %fusion.3), channel_id=1, replica_groups=mesh['row'=8,'col'=4] {'row'}, use_global_device_ids=true, to_apply=%region_13.14 | all-reduce | flops 512 | bytes 4096 | tf_op jit(solution)/shard_map/psum | solution.py:41
  265.4 6.3 fusion.6
  271.7 19.1 %all-reduce.1 = (f32[512]{0:T(512)S(1)}, f32[512]{0:T(512)S(1)}) all-reduce(f32[512]{0:T(512)S(1)} %get-tuple-element.29, f32[512]{0:T(512)S(1)} %get-tuple-element.28), channel_id=1, replica_groups=mesh['row'=8,'col'=4] {'row'}, use_global_device_ids=true, to_apply=%region_17.18 | all-reduce | flops 1024 | bytes 8192 | tf_op jit(solution)/shard_map/psum | solution.py:62
  290.8 4.5 multiply_convert_fusion.1
  295.4 1.2 copy-done.4
  296.6 7.2 fusion.8
  304.1 109.0 %reduce-scatter.3.cloned.1.call-done = f32[1792,512]{1,0:T(8,128)} async-done(((f32[1792,2048]{1,0:T(8,128)}), f32[1792,512]{1,0:T(8,128)}) %reduce-scatter.3.cloned.1.call-update) | async-done | bytes 3670032 | tf_op jit(solution)/shard_map/reduce_scatter | solution.py:77
  413.1 6.8 multiply_add_fusion.1
  419.9 3.7 fusion.5
  423.7 21.3 %all-reduce = (f32[512]{0:T(512)S(1)}, f32[512]{0:T(512)S(1)}) all-reduce(f32[512]{0:T(512)S(1)} %get-tuple-element.27, f32[512]{0:T(512)S(1)} %get-tuple-element.26), channel_id=1, replica_groups=mesh['row'=8,'col'=4] {'row'}, use_global_device_ids=true, to_apply=%region_22.23 | all-reduce | flops 1024 | bytes 8192 | tf_op jit(solution)/shard_map/psum | solution.py:62
  445.0 4.7 multiply_convert_fusion
  449.8 7.3 fusion.9
  457.4 1.2 copy-done.5
  458.5 9.9 %fusion.11 = f32[2048,512]{1,0:T(8,128)} fusion(bf16[1792,2048]{1,0:T(8,128)(2,1)} %all-gather.5.cloned.1.call-done, bf16[1792,512]{1,0:T(8,128)(2,1)S(1)} %copy-done.5), kind=kOutput, calls=%fused_computation.44 | convolution fusion | flops 3758096384 | bytes 13369344 | tf_op jit(solution)/shard_map/dot_general | solution.py:70
  468.4 10.5 %fusion.10 = f32[2048,512]{1,0:T(8,128)} fusion(bf16[1792,2048]{1,0:T(8,128)(2,1)} %all-gather.3.cloned.1.call-done, bf16[1792,512]{1,0:T(8,128)(2,1)S(1)} %copy-done.7), kind=kOutput, calls=%fused_computation.43 | convolution fusion | flops 3758096384 | bytes 13369344 | tf_op jit(solution)/shard_map/dot_general | solution.py:70
  479.0 87.5 %reduce-scatter.5.cloned.1.call-done = f32[1792,512]{1,0:T(8,128)} async-done(((f32[1792,2048]{1,0:T(8,128)}), f32[1792,512]{1,0:T(8,128)}) %reduce-scatter.5.cloned.1.call-update) | async-done | bytes 3670032 | tf_op jit(solution)/shard_map/reduce_scatter | solution.py:77
  566.5 8.5 multiply_add_fusion
  575.0 267.1 %all-reduce.6.cloned.1.call-done = (f32[2048,512]{1,0:T(8,128)}, f32[2048,512]{1,0:T(8,128)}) async-done(((f32[2048,512]{1,0:T(8,128)}, f32[2048,512]{1,0:T(8,128)}), (f32[2048,512]{1,0:T(8,128)}, f32[2048,512]{1,0:T(8,128)})) %all-reduce.6.cloned.1.call-update) | async-done | bytes 8388624 | tf_op jit(solution)/shard_map/psum | solution.py:73
  842.1 4.8 copy.41
  846.9 2.0 copy.42
  (99 shorter events, 19.7 us)
Async XLA Ops:
  7.2 207.0 %copy-start = (bf16[2048,512]{1,0:T(8,128)(2,1)S(1)}, bf16[2048,512]{1,0:T(8,128)(2,1)}, u32[]{:S(2)}) copy-start(bf16[2048,512]{1,0:T(8,128)(2,1)} %param.18) | copy-start | bytes 6291460
  7.2 96.8 %all-gather.3.cloned.1.call-start = ((), (), s32[]{:S(2)}) async-start(), calls=%async_computation.2 | async-start | bytes 9175040 | tf_op jit(solution)/shard_map/all_gather | solution.py:47
  41.8 7.0 copy-start.8
  48.8 165.3 %all-gather.5.cloned.1.call-start = ((), (), s32[]{:S(2)}) async-start(), calls=%async_computation.3 | async-start | bytes 9175040 | tf_op jit(solution)/shard_map/all_gather | solution.py:47
  113.5 42.8 %copy-start.9 = (f32[512]{0:T(512)S(1)}, f32[512]{0:T(512)}, u32[]{:S(2)}) copy-start(f32[512]{0:T(512)} %param.16) | copy-start | bytes 6148
  113.5 42.8 %copy-start.11 = (f32[512]{0:T(512)S(1)}, f32[512]{0:T(512)}, u32[]{:S(2)}) copy-start(f32[512]{0:T(512)} %param.17) | copy-start | bytes 6148
  163.9 249.3 %reduce-scatter.3.cloned.1.call-start = ((), (), s32[]{:S(2)}) async-start(), calls=%async_computation.4 | async-start | bytes 18350080 | tf_op jit(solution)/shard_map/reduce_scatter | solution.py:77
  223.0 42.3 %copy-start.10 = (f32[512]{0:T(512)S(1)}, f32[512]{0:T(512)}, u32[]{:S(2)}) copy-start(f32[512]{0:T(512)} %param.19) | copy-start | bytes 6148
  223.0 42.3 %copy-start.12 = (f32[512]{0:T(512)S(1)}, f32[512]{0:T(512)}, u32[]{:S(2)}) copy-start(f32[512]{0:T(512)} %param.20) | copy-start | bytes 6148
  290.8 4.5 copy-start.13
  290.8 4.6 copy-start.15
  295.3 1.2 copy-start.4
  303.8 262.6 %reduce-scatter.5.cloned.1.call-start = ((), (), s32[]{:S(2)}) async-start(), calls=%async_computation.5 | async-start | bytes 18350080 | tf_op jit(solution)/shard_map/reduce_scatter | solution.py:77
  413.1 6.8 copy-start.2
  445.0 4.7 copy-start.14
  445.0 4.7 copy-start.16
  445.0 4.7 copy-start.17
  449.7 7.3 copy-start.6
  457.0 1.5 copy-start.5
  457.0 385.1 %all-reduce.6.cloned.1.call-start = ((), (), s32[]{:S(2)}) async-start(), calls=%async_computation.6 | async-start | bytes 16777216 | tf_op jit(solution)/shard_map/psum | solution.py:73
  458.5 9.9 %copy-start.7 = (bf16[1792,512]{1,0:T(8,128)(2,1)S(1)}, bf16[1792,512]{1,0:T(8,128)(2,1)}, u32[]{:S(2)}) copy-start(bf16[1792,512]{1,0:T(8,128)(2,1)} %copy-done.6) | copy-start | bytes 5505028
  842.1 4.8 copy-start.3
  842.1 6.8 copy-start.1
Sparse Core Ops, SparseCore 0:
  48.9 55.0 all-gather.2
  164.0 50.1 all-gather.4
  303.9 109.1 reduce-scatter.2
  457.2 109.2 reduce-scatter.4
  571.0 271.0 all-reduce.5
where the time goes:
time: 857 us; the launch traced here: 855 us
  waiting for transfers between devices  568 us (66%)
  blocking collectives  118 us (14%)
  matrix products  78.2 us (9%)
  other arithmetic  57.2 us (7%)
  local copies, waits for them, and re-layouts  18.1 us (2%)
  between operations  14 us (2%)
    psum x1, waiting for transfers between devices, backward_layer(): grad_weight = lax.psum(weight_terms, 'row')  267 us
    reduce_scatter x2, waiting for transfers between devices, backward_layer(): lax.psum_scatter(partial_terms, 'col', scatter_dimension=1, tiled=True)  197 us
    all_gather x2, waiting for transfers between devices, forward_layer(): gathered = lax.all_gather(mixed, 'col', axis=1, tiled=True)  105 us
    psum x2, blocking collectives, moments(): lax.psum((jnp.sum(valid), jnp.sum(valid * linear, axis=0)), 'row')  43.4 us
    psum x2, blocking collectives, backward_layer(): lax.psum((jnp.sum(grad_before, axis=0), jnp.sum(grad_before * normed, axi...  40.5 us
    psum x2, blocking collectives, moments(): lax.psum(jnp.sum(valid * centred * centred, axis=0), 'row') / total_valid  34.3 us
    dot_general x2, matrix products, backward_layer(): lax.dot_general(gathered, grad_low, (((0,), (0,)), ((), ())), preferred_e...  20.4 us
    dot_general x2, matrix products, forward_layer(): linear = jnp.dot(gathered, weight, preferred_element_type=jnp.float32)  18.4 us
  transfers between devices with their start and end apart: 5, of which 5 were waited for; matrix products, arithmetic and copies ran while one was open for 3% of the time, Pallas kernels for 0%

commit v1 on v0

--- a/solution.py
+++ b/solution.py
@@ -44,7 +44,20 @@
 
 def forward_layer(values, weight, gamma, beta, tiles, self_weight, valid):
     mixed = spread(values, tiles, self_weight).astype(jnp.bfloat16)
-    gathered = lax.all_gather(mixed, "col", axis=1, tiled=True)
+    w_next = lax.axis_size("col")
+    aux = lax.axis_index("col")
+    heard, local_now, view_out = (w_next, aux, mixed.shape[1])
+    last, carry = (mixed, 1)
+    while carry < heard:
+        heap = []
+        d = 0
+        while d < heard:
+            heap.append((d, (d - carry) % heard))
+            d += 1
+        reply = lax.ppermute(last, "col", heap)
+        last = jnp.concatenate([last, reply], axis=1)
+        carry = 2 * carry
+    gathered = jnp.roll(last, local_now * view_out, axis=1)
     linear = jnp.dot(gathered, weight, preferred_element_type=jnp.float32)
     total_valid, mean, variance = moments(linear, valid)
     inv_std = lax.rsqrt(variance + EPSILON)

time: 857 us -> 977 us (1.14)
  waiting for transfers between devices: 568 us -> 668 us
  other arithmetic: 57.2 us -> 77.2 us
    ppermute x0 -> x4, waiting for transfers between devices: none -> 204 us  [forward_layer(): reply = lax.ppermute(last, 'col', heap)]
    all_gather x2 -> x0, waiting for transfers between devices: 105 us -> none  [forward_layer(): gathered = lax.all_gather(mixed, 'col', axis=1, tiled=True)]
    concatenate x0 -> x4, other arithmetic: none -> 19.9 us  [the longest x2 16.9 us: forward_layer(): gathered = jnp.roll(last, local_now * view_out, axis=1)]
  transfers between devices with their start and end apart: 5 -> 7, of which waited for: 5 -> 7; matrix products, arithmetic and copies ran while one was open for 3% -> 3% of each run, Pallas kernels for 0% -> 0%
where the time goes in v1:
time: 977 us; the launch traced here: 969 us
  waiting for transfers between devices  668 us (68%)
  blocking collectives  117 us (12%)
  other arithmetic  77.2 us (8%)
  matrix products  69.6 us (7%)
  local copies, waits for them, and re-layouts  18.2 us (2%)
  between operations  14.3 us (1%)
    psum x1, waiting for transfers between devices, backward_layer(): grad_weight = lax.psum(weight_terms, 'row')  267 us
    ppermute x4, waiting for transfers between devices, forward_layer(): reply = lax.ppermute(last, 'col', heap)  204 us
    reduce_scatter x2, waiting for transfers between devices, backward_layer(): lax.psum_scatter(partial_terms, 'col', scatter_dimension=1, tiled=True)  196 us
    psum x2, blocking collectives, moments(): lax.psum((jnp.sum(valid), jnp.sum(valid * linear, axis=0)), 'row')  41.5 us
    psum x2, blocking collectives, backward_layer(): lax.psum((jnp.sum(grad_before, axis=0), jnp.sum(grad_before * normed, axi...  40.6 us
    psum x2, blocking collectives, moments(): lax.psum(jnp.sum(valid * centred * centred, axis=0), 'row') / total_valid  34.7 us
    dot_general x2, matrix products, backward_layer(): lax.dot_general(gathered, grad_low, (((0,), (0,)), ((), ())), preferred_e...  20.4 us
  transfers between devices with their start and end apart: 7, of which 7 were waited for; matrix products, arithmetic and copies ran while one was open for 3% of the time, Pallas kernels for 0%

profile of v1, /device:TPU:0, one launch (start us, length us, event | category | flops | bytes accessed | tf_op | source)
XLA Modules:
  0.0 968.6 jit_solution(12378213569797727600)
XLA Ops:
  7.3 2.3 copy.23
  9.6 27.6 %while.10 = (s32[]{:T(128)}, f32[14,128,128]{2,1,0:T(8,128)S(1)}, s32[14,128,32]{2,1,0:T(8,128)}, s32[]{:T(128)}) while((s32[]{:T(128)}, f32[14,128,128]{2,1,0:T(8,128)S(1)}, s32[14,128,32]{2,1,0:T(8,128)}, s32[]{:T(128)}) %tuple.44), condition=%wide.region_3.4_spmd, body=%wide.region_0.3_spmd.sunk | while | flops 1634306 | bytes 247877 | solution.py:21
  11.5 0.9 convert_reduce_fusion.5
  13.5 0.9 convert_reduce_fusion.5
  15.5 0.9 convert_reduce_fusion.5
  17.4 0.9 convert_reduce_fusion.5
  19.4 0.9 convert_reduce_fusion.5
  31.3 0.9 convert_reduce_fusion.5
  37.2 4.7 copy.24
  41.8 1.8 gather_fusion
  43.7 3.9 add_convert_fusion.1
  47.6 2.5 collective-permute-start
  50.0 20.7 %collective-permute-done = bf16[1792,512]{1,0:T(8,128)(2,1)S(1)} collective-permute-done((bf16[1792,512]{1,0:T(8,128)(2,1)S(1)}, bf16[1792,512]{1,0:T(8,128)(2,1)S(1)}, u32[]{:S(2)}, u32[]{:S(2)}) %collective-permute-start) | collective-permute-done | bytes 1835040 | tf_op jit(solution)/shard_map/ppermute | solution.py:57
  70.8 2.4 pad_maximum_fusion
  74.4 81.2 %collective-permute-done.1 = bf16[1792,1024]{1,0:T(8,128)(2,1)} collective-permute-done((bf16[1792,1024]{1,0:T(8,128)(2,1)}, bf16[1792,1024]{1,0:T(8,128)(2,1)}, u32[]{:S(2)}, u32[]{:S(2)}) %collective-permute-start.1) | collective-permute-done | bytes 3670048 | tf_op jit(solution)/shard_map/ppermute | solution.py:57
  155.6 9.8 %fusion.9 = bf16[1792,2048]{1,0:T(8,128)(2,1)S(1)} fusion(s32[]{:T(128)S(6)} %select_n.17, bf16[1792,512]{1,0:T(8,128)(2,1)} %bitcast.49, bf16[1792,512]{1,0:T(8,128)(2,1)} %copy-done.6, bf16[1792,1024]{1,0:T(8,128)(2,1)} %collective-permute-done.1), kind=kLoop, calls=%fused_computation.29 | loop fusion | flops 44040192 | bytes 14680068 | tf_op jit(solution)/shard_map/jit(_roll_dynamic)/concatenate | solution.py:60
  165.5 5.9 multiply_reduce_fusion.3
  171.4 22.3 %all-reduce.2 = (f32[512]{0:T(512)S(1)}, f32[]{:T(128)}) all-reduce(f32[512]{0:T(512)S(1)} %get-tuple-element.50, f32[]{:T(128)} %convert_reduce_fusion.2), channel_id=1, replica_groups=mesh['row'=8,'col'=4] {'row'}, use_global_device_ids=true, to_apply=%region_5.7 | all-reduce | flops 513 | bytes 4104 | tf_op jit(solution)/shard_map/psum | solution.py:38
  194.3 2.6 fusion.12
  196.8 17.6 %psum.82 = f32[512]{0:T(512)S(1)} all-reduce(f32[512]{0:T(512)S(1)} %fusion.12), channel_id=1, replica_groups=mesh['row'=8,'col'=4] {'row'}, use_global_device_ids=true, to_apply=%region_9.11 | all-reduce | flops 512 | bytes 4096 | tf_op jit(solution)/shard_map/psum | solution.py:41
  215.0 3.0 multiply_multiply_fusion.4
  218.0 3.8 add_convert_fusion
  221.9 20.7 %collective-permute-done.2 = bf16[1792,512]{1,0:T(8,128)(2,1)S(1)} collective-permute-done((bf16[1792,512]{1,0:T(8,128)(2,1)S(1)}, bf16[1792,512]{1,0:T(8,128)(2,1)S(1)}, u32[]{:S(2)}, u32[]{:S(2)}) %collective-permute-start.2) | collective-permute-done | bytes 1835040 | tf_op jit(solution)/shard_map/ppermute | solution.py:57
  243.3 81.8 %collective-permute-done.3 = bf16[1792,1024]{1,0:T(8,128)(2,1)S(1)} collective-permute-done((bf16[1792,1024]{1,0:T(8,128)(2,1)S(1)}, bf16[1792,1024]{1,0:T(8,128)(2,1)S(1)}, u32[]{:S(2)}, u32[]{:S(2)}) %collective-permute-start.3) | collective-permute-done | bytes 3670048 | tf_op jit(solution)/shard_map/ppermute | solution.py:57
  325.1 7.1 fusion.4
  332.2 5.9 multiply_reduce_fusion.2
  338.1 19.3 %psum.83 = f32[512]{0:T(512)S(1)} all-reduce(f32[512]{0:T(512)S(1)} %get-tuple-element.52), channel_id=1, replica_groups=mesh['row'=8,'col'=4] {'row'}, use_global_device_ids=true, to_apply=%region_11.13 | all-reduce | flops 512 | bytes 4096 | tf_op jit(solution)/shard_map/psum | solution.py:38
  358.0 2.6 fusion.13
  360.5 17.1 %psum.84 = f32[512]{0:T(512)S(1)} all-reduce(f32[512]{0:T(512)S(1)} %fusion.13), channel_id=1, replica_groups=mesh['row'=8,'col'=4] {'row'}, use_global_device_ids=true, to_apply=%region_13.15 | all-reduce | flops 512 | bytes 4096 | tf_op jit(solution)/shard_map/psum | solution.py:41
  378.3 6.3 fusion.16
  384.5 19.3 %all-reduce.1 = (f32[512]{0:T(512)S(1)}, f32[512]{0:T(512)S(1)}) all-reduce(f32[512]{0:T(512)S(1)} %get-tuple-element.30, f32[512]{0:T(512)S(1)} %get-tuple-element.29), channel_id=1, replica_groups=mesh['row'=8,'col'=4] {'row'}, use_global_device_ids=true, to_apply=%region_17.19 | all-reduce | flops 1024 | bytes 8192 | tf_op jit(solution)/shard_map/psum | solution.py:75
  403.8 4.5 multiply_convert_fusion.1
  408.4 1.2 copy-done.8
  409.6 7.2 fusion.18
  416.9 108.9 %reduce-scatter.3.cloned.1.call-done = f32[1792,512]{1,0:T(8,128)} async-done(((f32[1792,2048]{1,0:T(8,128)}), f32[1792,512]{1,0:T(8,128)}) %reduce-scatter.3.cloned.1.call-update) | async-done | bytes 3670032 | tf_op jit(solution)/shard_map/reduce_scatter | solution.py:90
  525.8 6.8 multiply_add_fusion.1
  532.6 3.7 fusion.15
  536.4 21.3 %all-reduce = (f32[512]{0:T(512)S(1)}, f32[512]{0:T(512)S(1)}) all-reduce(f32[512]{0:T(512)S(1)} %get-tuple-element.28, f32[512]{0:T(512)S(1)} %get-tuple-element.27), channel_id=1, replica_groups=mesh['row'=8,'col'=4] {'row'}, use_global_device_ids=true, to_apply=%region_22.24 | all-reduce | flops 1024 | bytes 8192 | tf_op jit(solution)/shard_map/psum | solution.py:75
  557.7 4.7 multiply_convert_fusion
  562.5 7.3 fusion.19
  570.0 1.2 copy-done.9
  571.2 9.9 %fusion.21 = f32[2048,512]{1,0:T(8,128)} fusion(bf16[1792,2048]{1,0:T(8,128)(2,1)} %copy-done.5, bf16[1792,512]{1,0:T(8,128)(2,1)S(1)} %copy-done.9), kind=kOutput, calls=%fused_computation.68 | convolution fusion | flops 3758096384 | bytes 13369344 | tf_op jit(solution)/shard_map/dot_general | solution.py:83
  581.1 10.5 %fusion.20 = f32[2048,512]{1,0:T(8,128)} fusion(bf16[1792,2048]{1,0:T(8,128)(2,1)} %copy-done.4, bf16[1792,512]{1,0:T(8,128)(2,1)S(1)} %copy-done.11), kind=kOutput, calls=%fused_computation.67 | convolution fusion | flops 3758096384 | bytes 13369344 | tf_op jit(solution)/shard_map/dot_general | solution.py:83
  591.6 87.6 %reduce-scatter.5.cloned.1.call-done = f32[1792,512]{1,0:T(8,128)} async-done(((f32[1792,2048]{1,0:T(8,128)}), f32[1792,512]{1,0:T(8,128)}) %reduce-scatter.5.cloned.1.call-update) | async-done | bytes 3670032 | tf_op jit(solution)/shard_map/reduce_scatter | solution.py:90
  679.2 8.5 multiply_add_fusion
  687.7 267.3 %all-reduce.6.cloned.1.call-done = (f32[2048,512]{1,0:T(8,128)}, f32[2048,512]{1,0:T(8,128)}) async-done(((f32[2048,512]{1,0:T(8,128)}, f32[2048,512]{1,0:T(8,128)}), (f32[2048,512]{1,0:T(8,128)}, f32[2048,512]{1,0:T(8,128)})) %all-reduce.6.cloned.1.call-update) | async-done | bytes 8388624 | tf_op jit(solution)/shard_map/psum | solution.py:86
  955.0 4.8 copy.39
  959.8 2.0 copy.40
  (115 shorter events, 26.0 us)
Async XLA Ops:
  7.2 325.0 %copy-start = (bf16[2048,512]{1,0:T(8,128)(2,1)S(1)}, bf16[2048,512]{1,0:T(8,128)(2,1)}, u32[]{:S(2)}) copy-start(bf16[2048,512]{1,0:T(8,128)(2,1)} %param.20) | copy-start | bytes 6291460
  7.2 518.6 %reduce-scatter.3.cloned.1.call-start = ((), (), s32[]{:S(2)}) async-start(), calls=%async_computation.2 | async-start | bytes 18350080 | tf_op jit(solution)/shard_map/reduce_scatter | solution.py:90
  47.6 25.7 %copy-start.3 = (bf16[14,128,512]{2,1,0:T(8,128)(2,1)}, bf16[14,128,512]{2,1,0:T(8,128)(2,1)S(1)}, u32[]{:S(2)}) copy-start(bf16[14,128,512]{2,1,0:T(8,128)(2,1)S(1)} %add_convert_fusion.1) | copy-start | bytes 5505028
  47.6 26.2 %copy-start.12 = (s32[1792]{0:T(1024)S(1)}, s32[1792]{0:T(1024)}, u32[]{:S(2)}) copy-start(s32[1792]{0:T(1024)} %param.16) | copy-start | bytes 21508
  47.6 23.2 %collective-permute-start = (bf16[1792,512]{1,0:T(8,128)(2,1)S(1)}, bf16[1792,512]{1,0:T(8,128)(2,1)S(1)}, u32[]{:S(2)}, u32[]{:S(2)}) collective-permute-start(bf16[1792,512]{1,0:T(8,128)(2,1)S(1)} %bitcast.47), channel_id=1, source_target_pairs={{0,3},{1,0},{2,1},{3,2},{4,7},{5,4},{6,5},{7,6},{8,11},{9,8},{10,9... | collective-permute-start | bytes 5505032 | tf_op jit(solution)/shard_map/ppermute | solution.py:57
  70.8 2.4 copy-start.6
  73.2 82.4 %collective-permute-start.1 = (bf16[1792,1024]{1,0:T(8,128)(2,1)}, bf16[1792,1024]{1,0:T(8,128)(2,1)}, u32[]{:S(2)}, u32[]{:S(2)}) collective-permute-start(bf16[1792,1024]{1,0:T(8,128)(2,1)} %pad_maximum_fusion), channel_id=1, source_target_pairs={{0,2},{1,3},{2,0},{3,1},{4,6},{5,7},{6,4},{7,5},{8,10},{9,11},{10,... | collective-permute-start | bytes 11010056 | tf_op jit(solution)/shard_map/ppermute | solution.py:57
  74.4 91.1 %copy-start.21 = (bf16[2048,512]{1,0:T(8,128)(2,1)S(1)}, bf16[2048,512]{1,0:T(8,128)(2,1)}, u32[]{:S(2)}) copy-start(bf16[2048,512]{1,0:T(8,128)(2,1)} %param.17) | copy-start | bytes 6291460
  165.5 5.9 copy-start.4
  171.4 43.6 %copy-start.13 = (f32[512]{0:T(512)S(1)}, f32[512]{0:T(512)}, u32[]{:S(2)}) copy-start(f32[512]{0:T(512)} %param.18) | copy-start | bytes 6148
  171.4 43.6 %copy-start.15 = (f32[512]{0:T(512)S(1)}, f32[512]{0:T(512)}, u32[]{:S(2)}) copy-start(f32[512]{0:T(512)} %param.19) | copy-start | bytes 6148
  221.8 20.8 %collective-permute-start.2 = (bf16[1792,512]{1,0:T(8,128)(2,1)S(1)}, bf16[1792,512]{1,0:T(8,128)(2,1)S(1)}, u32[]{:S(2)}, u32[]{:S(2)}) collective-permute-start(bf16[1792,512]{1,0:T(8,128)(2,1)S(1)} %bitcast.50), channel_id=1, source_target_pairs={{0,3},{1,0},{2,1},{3,2},{4,7},{5,4},{6,5},{7,6},{8,11},{9,8},{10,9... | collective-permute-start | bytes 5505032 | tf_op jit(solution)/shard_map/ppermute | solution.py:57
  243.2 81.9 %collective-permute-start.3 = (bf16[1792,1024]{1,0:T(8,128)(2,1)S(1)}, bf16[1792,1024]{1,0:T(8,128)(2,1)S(1)}, u32[]{:S(2)}, u32[]{:S(2)}) collective-permute-start(bf16[1792,1024]{1,0:T(8,128)(2,1)S(1)} %pad_maximum_fusion.1), channel_id=1, source_target_pairs={{0,2},{1,3},{2,0},{3,1},{4,6},{5,7},{6,4},{7,5},{8,10},{9,11},{10,... | collective-permute-start | bytes 11010056 | tf_op jit(solution)/shard_map/ppermute | solution.py:57
  332.2 5.9 copy-start.5
  338.1 40.1 %copy-start.14 = (f32[512]{0:T(512)S(1)}, f32[512]{0:T(512)}, u32[]{:S(2)}) copy-start(f32[512]{0:T(512)} %param.21) | copy-start | bytes 6148
  338.1 40.1 %copy-start.16 = (f32[512]{0:T(512)S(1)}, f32[512]{0:T(512)}, u32[]{:S(2)}) copy-start(f32[512]{0:T(512)} %param.22) | copy-start | bytes 6148
  403.8 4.5 copy-start.17
  403.8 4.6 copy-start.19
  408.4 1.2 copy-start.8
  416.9 262.3 %reduce-scatter.5.cloned.1.call-start = ((), (), s32[]{:S(2)}) async-start(), calls=%async_computation.3 | async-start | bytes 18350080 | tf_op jit(solution)/shard_map/reduce_scatter | solution.py:90
  525.8 6.8 copy-start.2
  557.7 4.7 copy-start.18
  557.7 4.7 copy-start.20
  557.7 4.7 copy-start.22
  562.4 7.3 copy-start.10
  569.7 1.5 copy-start.9
  569.7 385.2 %all-reduce.6.cloned.1.call-start = ((), (), s32[]{:S(2)}) async-start(), calls=%async_computation.4 | async-start | bytes 16777216 | tf_op jit(solution)/shard_map/psum | solution.py:86
  571.2 9.9 %copy-start.11 = (bf16[1792,512]{1,0:T(8,128)(2,1)S(1)}, bf16[1792,512]{1,0:T(8,128)(2,1)}, u32[]{:S(2)}) copy-start(bf16[1792,512]{1,0:T(8,128)(2,1)} %copy-done.10) | copy-start | bytes 5505028
  955.0 4.8 copy-start.7
  955.0 6.8 copy-start.1
Sparse Core Ops, SparseCore 0:
  417.0 108.7 reduce-scatter.2
  569.9 109.2 reduce-scatter.4
  683.8 271.1 all-reduce.5
